TPU v7x, 256 devices: a whole 4x4x8 slice. The times are simulated.
256 devices in a mesh: prog: 32 (over z, x), clus: 8 (over y, core).
Axes of the slice: x: 4, y: 4, z: 8, core: 2. Of those that a mesh axis runs over, the one named last changes fastest.
Arguments:
- embeddings: bfloat16 [32768, 2048], P('prog', 'clus'), may hold values from -64 to 64, as said below
- centroids: bfloat16 [4096, 2048], P('clus'), may hold values from -6 to 6, as said below
- plan_grad: bfloat16 [32768, 4096], P('prog', 'clus'), may hold values from -24 to 24
Outputs:
- embed_grad: bfloat16 [32768, 2048], P('prog', 'clus')
- centroid_grad: bfloat16 [4096, 2048], P(('clus', 'prog'))
Inputs may be any that keep to these rules, and one draw needn't show every extreme that they name: embeddings are real-valued with full-rank spread. centroids are real-valued with full-rank spread.
All inputs are finite; a program needn't handle non-finite values.
Results may differ from a plain program's by a relative error of at most 0.006.
Values may be sent and summed in bfloat16 or wider, within the bound.
No kernel may reach another device: no remote copies, remote signals or barrier semaphores. Data moves between devices by JAX's collectives and lax.ppermute only.
A program may use at most 64 MiB of HBM per device.

v0:
```python
import jax
import jax.numpy as jnp
from jax import lax
from jax.sharding import PartitionSpec as P

D = 2048
CENTROIDS = 4096
ITERS = 4


def row_lse(values):
    top = lax.pmax(jnp.max(values, axis=1), "clus")
    total = lax.psum(jnp.sum(jnp.exp(values - top[:, None]), axis=1), "clus")
    return top + jnp.log(total)


def col_lse(values):
    top = lax.pmax(jnp.max(values, axis=0), "prog")
    total = lax.psum(jnp.sum(jnp.exp(values - top[None, :]), axis=0), "prog")
    return top + jnp.log(total)


def shards(embeddings, centroids, plan_grad):
    scale = 1.0 / (0.25 * jnp.sqrt(jnp.float32(D)))
    whole_rows = lax.all_gather(embeddings, "clus", axis=1, tiled=True)
    logits = scale * lax.dot_general(
        whole_rows, centroids, (((1,), (1,)), ((), ())), preferred_element_type=jnp.float32
    )
    total_rows = embeddings.shape[0] * lax.axis_size("prog")
    log_b = jnp.log(jnp.float32(total_rows) / jnp.float32(CENTROIDS))
    col_pot = jnp.zeros((centroids.shape[0],), jnp.float32)
    row_list = []
    col_list = []
    for step in range(ITERS):
        row_pot = -row_lse(logits + col_pot[None, :])
        col_pot = log_b - col_lse(logits + row_pot[:, None])
        row_list.append(row_pot)
        col_list.append(col_pot)
    plan = jnp.exp(logits + row_list[-1][:, None] + col_list[-1][None, :])
    pbar = plan_grad.astype(jnp.float32) * plan
    adjoint = pbar
    col_adj = lax.psum(jnp.sum(pbar, axis=0), "prog")
    direct = jnp.sum(pbar, axis=1)
    for step in range(ITERS - 1, -1, -1):
        weights_a = jnp.exp(logits + row_list[step][:, None] + col_list[step][None, :] - log_b)
        term_a = weights_a * col_adj[None, :]
        adjoint = adjoint - term_a
        row_adj = lax.psum(direct - jnp.sum(term_a, axis=1), "clus")
        direct = jnp.zeros_like(direct)
        if step > 0:
            prev_col = col_list[step - 1]
        else:
            prev_col = jnp.zeros_like(col_pot)
        term_b = jnp.exp(logits + prev_col[None, :] + row_list[step][:, None]) * row_adj[:, None]
        adjoint = adjoint - term_b
        if step > 0:
            col_adj = -lax.psum(jnp.sum(term_b, axis=0), "prog")
    adjoint_b = adjoint.astype(jnp.bfloat16)
    partial_rows = scale * jnp.dot(adjoint_b, centroids, preferred_element_type=jnp.float32)
    embed_grad = lax.psum_scatter(partial_rows, "clus", scatter_dimension=1, tiled=True).astype(
        jnp.bfloat16
    )
    centroid_grad = lax.psum_scatter(
        scale
        * lax.dot_general(
            adjoint_b, whole_rows, (((0,), (0,)), ((), ())), preferred_element_type=jnp.float32
        ),
        "prog",
        scatter_dimension=0,
        tiled=True,
    ).astype(jnp.bfloat16)
    return (embed_grad, centroid_grad)


def solution(mesh):
    placed = (P("prog", "clus"), P("clus", None), P("prog", "clus"))
    return jax.shard_map(
        shards,
        mesh=mesh,
        in_specs=placed,
        out_specs=(P("prog", "clus"), P(("clus", "prog"), None)),
        check_vma=False,
    )
```

profile of v0, /device:TPU:1, one launch (start us, length us, event | category | flops | bytes accessed | tf_op | source)
XLA Modules:
  0.0 1400.4 jit_solution(5728778426446037416)
XLA Ops:
  9.5 42.7 %all-gather.2.cloned.1.call-done = bf16[1024,2048]{1,0:T(8,128)(2,1)} async-done(((bf16[1024,256]{1,0:T(8,128)(2,1)}), bf16[1024,2048]{1,0:T(8,128)(2,1)}) %all-gather.2.cloned.1.call-update) | async-done | bytes 4194320 | tf_op jit(solution)/shard_map/all_gather | solution.py:25
  52.1 5.9 fusion.9
  58.0 12.0 pmax.56
  70.0 1.9 exponential_reduce_fusion.7
  71.9 14.3 %psum.112 = f32[1024]{0:T(1024)S(1)} all-reduce(f32[1024]{0:T(1024)S(1)} %exponential_reduce_fusion.7), channel_id=1, replica_groups=mesh['prog'=32,'clus'=8] {'clus'}, use_global_device_ids=true, to_apply=%region_3.0 | all-reduce | flops 1024 | bytes 8192 | tf_op jit(solution)/shard_map/psum | solution.py:13
  88.1 60.9 %pmax.57 = f32[512]{0:T(512)S(1)} all-reduce(f32[512]{0:T(512)S(1)} %add_reduce_fusion.6), channel_id=1, replica_groups=mesh['prog'=32,'clus'=8] {'prog'}, use_global_device_ids=true, to_apply=%region_5.0 | all-reduce | flops 512 | bytes 4096 | tf_op jit(solution)/shard_map/pmax | solution.py:18
  148.9 2.1 exponential_reduce_fusion.6
  151.0 56.1 %psum.113 = f32[512]{0:T(512)S(1)} all-reduce(f32[512]{0:T(512)S(1)} %exponential_reduce_fusion.6), channel_id=1, replica_groups=mesh['prog'=32,'clus'=8] {'prog'}, use_global_device_ids=true, to_apply=%region_7.0 | all-reduce | flops 512 | bytes 4096 | tf_op jit(solution)/shard_map/psum | solution.py:19
  208.9 40.2 %pmax.58 = f32[1024]{0:T(1024)S(1)} all-reduce(f32[1024]{0:T(1024)S(1)} %add_reduce_fusion.4), channel_id=1, replica_groups=mesh['prog'=32,'clus'=8] {'clus'}, use_global_device_ids=true, to_apply=%region_9.0 | all-reduce | flops 1024 | bytes 8192 | tf_op jit(solution)/shard_map/pmax | solution.py:12
  249.1 2.0 exponential_reduce_fusion.5
  251.1 12.4 psum.114
  265.4 57.4 %pmax.59 = f32[512]{0:T(512)S(1)} all-reduce(f32[512]{0:T(512)S(1)} %add_reduce_fusion.3), channel_id=1, replica_groups=mesh['prog'=32,'clus'=8] {'prog'}, use_global_device_ids=true, to_apply=%region_13.0 | all-reduce | flops 512 | bytes 4096 | tf_op jit(solution)/shard_map/pmax | solution.py:18
  322.8 2.1 exponential_reduce_fusion.4
  324.9 56.1 %psum.115 = f32[512]{0:T(512)S(1)} all-reduce(f32[512]{0:T(512)S(1)} %exponential_reduce_fusion.4), channel_id=1, replica_groups=mesh['prog'=32,'clus'=8] {'prog'}, use_global_device_ids=true, to_apply=%region_15.0 | all-reduce | flops 512 | bytes 4096 | tf_op jit(solution)/shard_map/psum | solution.py:19
  382.9 40.1 %pmax.60 = f32[1024]{0:T(1024)S(1)} all-reduce(f32[1024]{0:T(1024)S(1)} %add_reduce_fusion.2), channel_id=1, replica_groups=mesh['prog'=32,'clus'=8] {'clus'}, use_global_device_ids=true, to_apply=%region_17.0 | all-reduce | flops 1024 | bytes 8192 | tf_op jit(solution)/shard_map/pmax | solution.py:12
  423.0 2.0 exponential_reduce_fusion.3
  425.0 12.4 psum.116
  439.2 57.4 %pmax.61 = f32[512]{0:T(512)S(1)} all-reduce(f32[512]{0:T(512)S(1)} %add_reduce_fusion.1), channel_id=1, replica_groups=mesh['prog'=32,'clus'=8] {'prog'}, use_global_device_ids=true, to_apply=%region_21.0 | all-reduce | flops 512 | bytes 4096 | tf_op jit(solution)/shard_map/pmax | solution.py:18
  496.7 2.1 exponential_reduce_fusion.2
  498.8 56.1 %psum.117 = f32[512]{0:T(512)S(1)} all-reduce(f32[512]{0:T(512)S(1)} %exponential_reduce_fusion.2), channel_id=1, replica_groups=mesh['prog'=32,'clus'=8] {'prog'}, use_global_device_ids=true, to_apply=%region_23.0 | all-reduce | flops 512 | bytes 4096 | tf_op jit(solution)/shard_map/psum | solution.py:19
  556.7 40.1 %pmax.62 = f32[1024]{0:T(1024)S(1)} all-reduce(f32[1024]{0:T(1024)S(1)} %add_reduce_fusion), channel_id=1, replica_groups=mesh['prog'=32,'clus'=8] {'clus'}, use_global_device_ids=true, to_apply=%region_25.0 | all-reduce | flops 1024 | bytes 8192 | tf_op jit(solution)/shard_map/pmax | solution.py:12
  596.8 2.0 exponential_reduce_fusion.1
  598.9 12.4 psum.118
  613.1 57.4 %pmax.63 = f32[512]{0:T(512)S(1)} all-reduce(f32[512]{0:T(512)S(1)} %add_reduce_fusion.5), channel_id=1, replica_groups=mesh['prog'=32,'clus'=8] {'prog'}, use_global_device_ids=true, to_apply=%region_29.0 | all-reduce | flops 512 | bytes 4096 | tf_op jit(solution)/shard_map/pmax | solution.py:18
  670.5 2.1 exponential_reduce_fusion
  672.6 56.2 %psum.119 = f32[512]{0:T(512)S(1)} all-reduce(f32[512]{0:T(512)S(1)} %exponential_reduce_fusion), channel_id=1, replica_groups=mesh['prog'=32,'clus'=8] {'prog'}, use_global_device_ids=true, to_apply=%region_31.0 | all-reduce | flops 512 | bytes 4096 | tf_op jit(solution)/shard_map/psum | solution.py:19
  728.8 2.3 fusion.8
  731.1 57.0 %psum.120 = f32[512]{0:T(512)S(1)} all-reduce(f32[512]{0:T(512)S(1)} %get-tuple-element.2), channel_id=1, replica_groups=mesh['prog'=32,'clus'=8] {'prog'}, use_global_device_ids=true, to_apply=%region_33.0 | all-reduce | flops 512 | bytes 4096 | tf_op jit(solution)/shard_map/psum | solution.py:42
  788.1 2.1 fusion.4
  790.3 54.7 %psum.121 = f32[1024]{0:T(1024)S(1)} all-reduce(f32[1024]{0:T(1024)S(1)} %sub.146), channel_id=1, replica_groups=mesh['prog'=32,'clus'=8] {'clus'}, use_global_device_ids=true, to_apply=%region_36.0 | all-reduce | flops 1024 | bytes 8192 | tf_op jit(solution)/shard_map/psum | solution.py:48
  845.0 2.2 fusion.1
  847.1 55.9 %psum.122 = f32[512]{0:T(512)S(1)} all-reduce(f32[512]{0:T(512)S(1)} %fusion.1), channel_id=1, replica_groups=mesh['prog'=32,'clus'=8] {'prog'}, use_global_device_ids=true, to_apply=%region_38.0 | all-reduce | flops 512 | bytes 4096 | tf_op jit(solution)/shard_map/psum | solution.py:57
  903.0 2.1 fusion.5
  905.2 26.4 %psum.123 = f32[1024]{0:T(1024)S(1)} all-reduce(f32[1024]{0:T(1024)S(1)} %broadcast_subtract_fusion.2), channel_id=1, replica_groups=mesh['prog'=32,'clus'=8] {'clus'}, use_global_device_ids=true, to_apply=%region_40.0 | all-reduce | flops 1024 | bytes 8192 | tf_op jit(solution)/shard_map/psum | solution.py:48
  931.6 2.2 fusion.2
  933.7 57.4 %psum.124 = f32[512]{0:T(512)S(1)} all-reduce(f32[512]{0:T(512)S(1)} %fusion.2), channel_id=1, replica_groups=mesh['prog'=32,'clus'=8] {'prog'}, use_global_device_ids=true, to_apply=%region_42.0 | all-reduce | flops 512 | bytes 4096 | tf_op jit(solution)/shard_map/psum | solution.py:57
  991.2 2.1 fusion.6
  993.3 26.6 %psum.125 = f32[1024]{0:T(1024)S(1)} all-reduce(f32[1024]{0:T(1024)S(1)} %broadcast_subtract_fusion.1), channel_id=1, replica_groups=mesh['prog'=32,'clus'=8] {'clus'}, use_global_device_ids=true, to_apply=%region_44.0 | all-reduce | flops 1024 | bytes 8192 | tf_op jit(solution)/shard_map/psum | solution.py:48
  1019.9 2.2 fusion.3
  1022.1 55.7 %psum.126 = f32[512]{0:T(512)S(1)} all-reduce(f32[512]{0:T(512)S(1)} %fusion.3), channel_id=1, replica_groups=mesh['prog'=32,'clus'=8] {'prog'}, use_global_device_ids=true, to_apply=%region_46.0 | all-reduce | flops 512 | bytes 4096 | tf_op jit(solution)/shard_map/psum | solution.py:57
  1077.8 2.1 fusion
  1080.0 26.4 %psum.127 = f32[1024]{0:T(1024)S(1)} all-reduce(f32[1024]{0:T(1024)S(1)} %broadcast_subtract_fusion), channel_id=1, replica_groups=mesh['prog'=32,'clus'=8] {'clus'}, use_global_device_ids=true, to_apply=%region_48.0 | all-reduce | flops 1024 | bytes 8192 | tf_op jit(solution)/shard_map/psum | solution.py:48
  1106.4 6.2 subtract_convert_fusion
  1113.6 4.3 convolution_multiply_fusion.1
  1119.2 5.6 convolution_multiply_fusion
  1124.8 206.5 %reduce-scatter.5.cloned.1.call-done = f32[16,2048]{1,0:T(8,128)} async-done(((f32[512,2048]{1,0:T(8,128)}), f32[16,2048]{1,0:T(8,128)}) %reduce-scatter.5.cloned.1.call-update) | async-done | bytes 131088 | tf_op jit(solution)/shard_map/reduce_scatter | solution.py:63
  1332.8 59.0 %reduce-scatter.3.cloned.1.call-done = f32[1024,256]{1,0:T(8,128)} async-done(((f32[1024,2048]{1,0:T(8,128)}), f32[1024,256]{1,0:T(8,128)}) %reduce-scatter.3.cloned.1.call-update) | async-done | bytes 1048592 | tf_op jit(solution)/shard_map/reduce_scatter | solution.py:60
  1391.8 2.1 convert_element_type.14
  (38 shorter events, 18.8 us)
Async XLA Ops:
  7.2 45.0 %copy-start = (bf16[512,2048]{1,0:T(8,128)(2,1)S(1)}, bf16[512,2048]{1,0:T(8,128)(2,1)}, u32[]{:S(2)}) copy-start(bf16[512,2048]{1,0:T(8,128)(2,1)} %param.4) | copy-start | bytes 6291460
  7.2 45.0 %all-gather.2.cloned.1.call-start = ((), (), s32[]{:S(2)}) async-start(), calls=%async_computation.2 | async-start | bytes 4718592 | tf_op jit(solution)/shard_map/all_gather | solution.py:25
  7.9 1323.4 %reduce-scatter.5.cloned.1.call-start = ((), (), s32[]{:S(2)}) async-start(), calls=%async_computation.4 | async-start | bytes 4325376 | tf_op jit(solution)/shard_map/reduce_scatter | solution.py:63
  1106.4 7.2 copy-start.1
  1112.6 1.0 copy-start.2
  1117.9 1.2 copy-start.3
  1118.0 273.8 %reduce-scatter.3.cloned.1.call-start = ((), (), s32[]{:S(2)}) async-start(), calls=%async_computation.3 | async-start | bytes 9437184 | tf_op jit(solution)/shard_map/reduce_scatter | solution.py:60
Sparse Core Ops, SparseCore 0:
  9.8 42.2 all-gather.1
  1118.1 213.1 reduce-scatter.4
  1333.8 57.9 reduce-scatter.2
where the time goes:
time: 1400 us
  blocking collectives  1000 us (71%)
  waiting for transfers between devices  309 us (22%)
  other arithmetic  56.3 us (4%)
  matrix products  15.8 us (1%)
    pmax x4, blocking collectives, col_lse(): top = lax.pmax(jnp.max(values, axis=0), 'prog')  233 us
    psum x4, blocking collectives, col_lse(): total = lax.psum(jnp.sum(jnp.exp(values - top[None, :]), axis=0), 'prog')  225 us
    reduce_scatter x1, waiting for transfers between devices, shards(): lax.psum_scatter(scale * lax.dot_general(adjoint_b, whole_rows, (((0,), (...  206 us
    psum x3, blocking collectives, shards(): col_adj = -lax.psum(jnp.sum(term_b, axis=0), 'prog')  169 us
    psum x4, blocking collectives, shards(): row_adj = lax.psum(direct - jnp.sum(term_a, axis=1), 'clus')  134 us
    pmax x4, blocking collectives, row_lse(): top = lax.pmax(jnp.max(values, axis=1), 'clus')  132 us
    reduce_scatter x1, waiting for transfers between devices, shards(): lax.psum_scatter(partial_rows, 'clus', scatter_dimension=1, tiled=True)  59 us
    psum x1, blocking collectives, shards(): col_adj = lax.psum(jnp.sum(pbar, axis=0), 'prog')  57 us
  transfers between devices with their start and end apart: 3, of which 3 were waited for; matrix products, arithmetic and copies ran while one was open for 1% of the time, Pallas kernels for 0%

commit v1 on v0

--- a/solution.py
+++ b/solution.py
@@ -16,7 +16,7 @@
 
 def col_lse(values):
     top = lax.pmax(jnp.max(values, axis=0), "prog")
-    total = lax.psum(jnp.sum(jnp.exp(values - top[None, :]), axis=0), "prog")
+    total = jnp.sum(lax.all_gather(jnp.sum(jnp.exp(values - top[None, :]), axis=0), "prog"), axis=0)
     return top + jnp.log(total)
 
 

time: 1400 us -> 1310 us (0.936)
  blocking collectives: 1000 us -> 909 us
    psum x4 -> x0, blocking collectives: 225 us -> none  [col_lse(): total = lax.psum(jnp.sum(jnp.exp(values - top[None, :]), axis=0), 'prog')]
    all_gather x0 -> x4, blocking collectives: none -> 134 us  [col_lse(): lax.all_gather(jnp.sum(jnp.exp(values - top[None, :]), axis=0), 'prog')]
where the time goes in v1:
time: 1310 us
  blocking collectives  909 us (69%)
  waiting for transfers between devices  309 us (24%)
  other arithmetic  56.6 us (4%)
  matrix products  15.8 us (1%)
  between operations  13.9 us (1%)
    pmax x4, blocking collectives, col_lse(): top = lax.pmax(jnp.max(values, axis=0), 'prog')  235 us
    reduce_scatter x1, waiting for transfers between devices, shards(): lax.psum_scatter(scale * lax.dot_general(adjoint_b, whole_rows, (((0,), (...  207 us
    psum x3, blocking collectives, shards(): col_adj = -lax.psum(jnp.sum(term_b, axis=0), 'prog')  169 us
    all_gather x4, blocking collectives, col_lse(): lax.all_gather(jnp.sum(jnp.exp(values - top[None, :]), axis=0), 'prog')  134 us
    psum x4, blocking collectives, shards(): row_adj = lax.psum(direct - jnp.sum(term_a, axis=1), 'clus')  132 us
    pmax x4, blocking collectives, row_lse(): top = lax.pmax(jnp.max(values, axis=1), 'clus')  128 us
    reduce_scatter x1, waiting for transfers between devices, shards(): lax.psum_scatter(partial_rows, 'clus', scatter_dimension=1, tiled=True)  58.5 us
    psum x1, blocking collectives, shards(): col_adj = lax.psum(jnp.sum(pbar, axis=0), 'prog')  58.1 us
  transfers between devices with their start and end apart: 3, of which 3 were waited for; matrix products, arithmetic and copies ran while one was open for 1% of the time, Pallas kernels for 0%

profile of v1, /device:TPU:1, one launch (start us, length us, event | category | flops | bytes accessed | tf_op | source)
XLA Modules:
  0.0 1307.6 jit_solution(8836760041979009753)
XLA Ops:
  9.5 42.7 %all-gather.10.cloned.1.call-done = bf16[1024,2048]{1,0:T(8,128)(2,1)} async-done(((bf16[1024,256]{1,0:T(8,128)(2,1)}), bf16[1024,2048]{1,0:T(8,128)(2,1)}) %all-gather.10.cloned.1.call-update) | async-done | bytes 4194320 | tf_op jit(solution)/shard_map/all_gather | solution.py:25
  52.1 5.9 fusion.9
  58.0 12.0 pmax.56
  70.0 1.9 exponential_reduce_fusion.7
  71.9 14.3 %psum.84 = f32[1024]{0:T(1024)S(1)} all-reduce(f32[1024]{0:T(1024)S(1)} %exponential_reduce_fusion.7), channel_id=1, replica_groups=mesh['prog'=32,'clus'=8] {'clus'}, use_global_device_ids=true, to_apply=%region_3.0 | all-reduce | flops 1024 | bytes 8192 | tf_op jit(solution)/shard_map/psum | solution.py:13
  88.1 60.9 %pmax.57 = f32[512]{0:T(512)S(1)} all-reduce(f32[512]{0:T(512)S(1)} %add_reduce_fusion.6), channel_id=1, replica_groups=mesh['prog'=32,'clus'=8] {'prog'}, use_global_device_ids=true, to_apply=%region_5.0 | all-reduce | flops 512 | bytes 4096 | tf_op jit(solution)/shard_map/pmax | solution.py:18
  148.9 2.1 exponential_reduce_fusion.6
  151.0 33.9 %all-gather.4 = f32[32,1,512]{2,1,0:T(1,128)S(1)} all-gather(f32[1,1,512]{2,1,0:T(1,128)S(1)} %bitcast.10), channel_id=2, replica_groups=mesh['prog'=32,'clus'=8] {'prog'}, dimensions={0}, use_global_device_ids=true | all-gather | bytes 67584 | tf_op jit(solution)/shard_map/all_gather | solution.py:19
  186.8 38.4 %pmax.58 = f32[1024]{0:T(1024)S(1)} all-reduce(f32[1024]{0:T(1024)S(1)} %add_reduce_fusion.4), channel_id=1, replica_groups=mesh['prog'=32,'clus'=8] {'clus'}, use_global_device_ids=true, to_apply=%region_9.0 | all-reduce | flops 1024 | bytes 8192 | tf_op jit(solution)/shard_map/pmax | solution.py:12
  225.2 2.0 exponential_reduce_fusion.5
  227.3 12.4 psum.85
  241.5 58.1 %pmax.59 = f32[512]{0:T(512)S(1)} all-reduce(f32[512]{0:T(512)S(1)} %add_reduce_fusion.3), channel_id=1, replica_groups=mesh['prog'=32,'clus'=8] {'prog'}, use_global_device_ids=true, to_apply=%region_13.0 | all-reduce | flops 512 | bytes 4096 | tf_op jit(solution)/shard_map/pmax | solution.py:18
  299.6 2.1 exponential_reduce_fusion.4
  301.7 33.5 %all-gather.5 = f32[32,1,512]{2,1,0:T(1,128)S(1)} all-gather(f32[1,1,512]{2,1,0:T(1,128)S(1)} %bitcast.11), channel_id=3, replica_groups=mesh['prog'=32,'clus'=8] {'prog'}, dimensions={0}, use_global_device_ids=true | all-gather | bytes 67584 | tf_op jit(solution)/shard_map/all_gather | solution.py:19
  337.1 38.8 %pmax.60 = f32[1024]{0:T(1024)S(1)} all-reduce(f32[1024]{0:T(1024)S(1)} %add_reduce_fusion.2), channel_id=1, replica_groups=mesh['prog'=32,'clus'=8] {'clus'}, use_global_device_ids=true, to_apply=%region_17.0 | all-reduce | flops 1024 | bytes 8192 | tf_op jit(solution)/shard_map/pmax | solution.py:12
  375.9 2.0 exponential_reduce_fusion.3
  377.9 12.4 psum.86
  392.2 58.1 %pmax.61 = f32[512]{0:T(512)S(1)} all-reduce(f32[512]{0:T(512)S(1)} %add_reduce_fusion.1), channel_id=1, replica_groups=mesh['prog'=32,'clus'=8] {'prog'}, use_global_device_ids=true, to_apply=%region_21.0 | all-reduce | flops 512 | bytes 4096 | tf_op jit(solution)/shard_map/pmax | solution.py:18
  450.3 2.1 exponential_reduce_fusion.2
  452.4 33.5 %all-gather.6 = f32[32,1,512]{2,1,0:T(1,128)S(1)} all-gather(f32[1,1,512]{2,1,0:T(1,128)S(1)} %bitcast.12), channel_id=4, replica_groups=mesh['prog'=32,'clus'=8] {'prog'}, dimensions={0}, use_global_device_ids=true | all-gather | bytes 67584 | tf_op jit(solution)/shard_map/all_gather | solution.py:19
  487.8 38.8 %pmax.62 = f32[1024]{0:T(1024)S(1)} all-reduce(f32[1024]{0:T(1024)S(1)} %add_reduce_fusion), channel_id=1, replica_groups=mesh['prog'=32,'clus'=8] {'clus'}, use_global_device_ids=true, to_apply=%region_25.0 | all-reduce | flops 1024 | bytes 8192 | tf_op jit(solution)/shard_map/pmax | solution.py:12
  526.6 2.0 exponential_reduce_fusion.1
  528.6 12.4 psum.87
  542.8 58.1 %pmax.63 = f32[512]{0:T(512)S(1)} all-reduce(f32[512]{0:T(512)S(1)} %add_reduce_fusion.5), channel_id=1, replica_groups=mesh['prog'=32,'clus'=8] {'prog'}, use_global_device_ids=true, to_apply=%region_29.0 | all-reduce | flops 512 | bytes 4096 | tf_op jit(solution)/shard_map/pmax | solution.py:18
  600.9 2.1 exponential_reduce_fusion
  603.0 33.5 %all-gather.7 = f32[32,1,512]{2,1,0:T(1,128)S(1)} all-gather(f32[1,1,512]{2,1,0:T(1,128)S(1)} %bitcast.13), channel_id=5, replica_groups=mesh['prog'=32,'clus'=8] {'prog'}, dimensions={0}, use_global_device_ids=true | all-gather | bytes 67584 | tf_op jit(solution)/shard_map/all_gather | solution.py:19
  636.6 2.3 fusion.8
  638.9 58.1 %psum.88 = f32[512]{0:T(512)S(1)} all-reduce(f32[512]{0:T(512)S(1)} %get-tuple-element.2), channel_id=1, replica_groups=mesh['prog'=32,'clus'=8] {'prog'}, use_global_device_ids=true, to_apply=%region_33.0 | all-reduce | flops 512 | bytes 4096 | tf_op jit(solution)/shard_map/psum | solution.py:42
  697.0 2.1 fusion.4
  699.2 53.1 %psum.89 = f32[1024]{0:T(1024)S(1)} all-reduce(f32[1024]{0:T(1024)S(1)} %sub.146), channel_id=1, replica_groups=mesh['prog'=32,'clus'=8] {'clus'}, use_global_device_ids=true, to_apply=%region_36.0 | all-reduce | flops 1024 | bytes 8192 | tf_op jit(solution)/shard_map/psum | solution.py:48
  752.3 2.2 fusion.1
  754.5 55.7 %psum.90 = f32[512]{0:T(512)S(1)} all-reduce(f32[512]{0:T(512)S(1)} %fusion.1), channel_id=1, replica_groups=mesh['prog'=32,'clus'=8] {'prog'}, use_global_device_ids=true, to_apply=%region_38.0 | all-reduce | flops 512 | bytes 4096 | tf_op jit(solution)/shard_map/psum | solution.py:57
  810.2 2.1 fusion.5
  812.4 26.3 %psum.91 = f32[1024]{0:T(1024)S(1)} all-reduce(f32[1024]{0:T(1024)S(1)} %broadcast_subtract_fusion.2), channel_id=1, replica_groups=mesh['prog'=32,'clus'=8] {'clus'}, use_global_device_ids=true, to_apply=%region_40.0 | all-reduce | flops 1024 | bytes 8192 | tf_op jit(solution)/shard_map/psum | solution.py:48
  838.7 2.2 fusion.2
  840.9 57.4 %psum.92 = f32[512]{0:T(512)S(1)} all-reduce(f32[512]{0:T(512)S(1)} %fusion.2), channel_id=1, replica_groups=mesh['prog'=32,'clus'=8] {'prog'}, use_global_device_ids=true, to_apply=%region_42.0 | all-reduce | flops 512 | bytes 4096 | tf_op jit(solution)/shard_map/psum | solution.py:57
  898.3 2.1 fusion.6
  900.5 26.6 %psum.93 = f32[1024]{0:T(1024)S(1)} all-reduce(f32[1024]{0:T(1024)S(1)} %broadcast_subtract_fusion.1), channel_id=1, replica_groups=mesh['prog'=32,'clus'=8] {'clus'}, use_global_device_ids=true, to_apply=%region_44.0 | all-reduce | flops 1024 | bytes 8192 | tf_op jit(solution)/shard_map/psum | solution.py:48
  927.1 2.2 fusion.3
  929.3 55.7 %psum.94 = f32[512]{0:T(512)S(1)} all-reduce(f32[512]{0:T(512)S(1)} %fusion.3), channel_id=1, replica_groups=mesh['prog'=32,'clus'=8] {'prog'}, use_global_device_ids=true, to_apply=%region_46.0 | all-reduce | flops 512 | bytes 4096 | tf_op jit(solution)/shard_map/psum | solution.py:57
  985.0 2.1 fusion
  987.2 26.3 %psum.95 = f32[1024]{0:T(1024)S(1)} all-reduce(f32[1024]{0:T(1024)S(1)} %broadcast_subtract_fusion), channel_id=1, replica_groups=mesh['prog'=32,'clus'=8] {'clus'}, use_global_device_ids=true, to_apply=%region_48.0 | all-reduce | flops 1024 | bytes 8192 | tf_op jit(solution)/shard_map/psum | solution.py:48
  1013.5 6.3 subtract_convert_fusion
  1020.8 4.3 convolution_multiply_fusion.1
  1026.3 5.6 convolution_multiply_fusion
  1032.0 206.9 %reduce-scatter.5.cloned.1.call-done = f32[16,2048]{1,0:T(8,128)} async-done(((f32[512,2048]{1,0:T(8,128)}), f32[16,2048]{1,0:T(8,128)}) %reduce-scatter.5.cloned.1.call-update) | async-done | bytes 131088 | tf_op jit(solution)/shard_map/reduce_scatter | solution.py:63
  1240.4 58.5 %reduce-scatter.3.cloned.1.call-done = f32[1024,256]{1,0:T(8,128)} async-done(((f32[1024,2048]{1,0:T(8,128)}), f32[1024,256]{1,0:T(8,128)}) %reduce-scatter.3.cloned.1.call-update) | async-done | bytes 1048592 | tf_op jit(solution)/shard_map/reduce_scatter | solution.py:60
  1299.0 2.1 convert_element_type.14
  (42 shorter events, 19.0 us)
Async XLA Ops:
  7.2 45.0 %copy-start = (bf16[512,2048]{1,0:T(8,128)(2,1)S(1)}, bf16[512,2048]{1,0:T(8,128)(2,1)}, u32[]{:S(2)}) copy-start(bf16[512,2048]{1,0:T(8,128)(2,1)} %param.4) | copy-start | bytes 6291460
  7.2 45.0 %all-gather.10.cloned.1.call-start = ((), (), s32[]{:S(2)}) async-start(), calls=%async_computation.2 | async-start | bytes 4718592 | tf_op jit(solution)/shard_map/all_gather | solution.py:25
  7.9 1231.0 %reduce-scatter.5.cloned.1.call-start = ((), (), s32[]{:S(2)}) async-start(), calls=%async_computation.4 | async-start | bytes 4325376 | tf_op jit(solution)/shard_map/reduce_scatter | solution.py:63
  1013.5 7.2 copy-start.1
  1019.8 1.0 copy-start.2
  1025.1 1.2 copy-start.3
  1025.1 273.8 %reduce-scatter.3.cloned.1.call-start = ((), (), s32[]{:S(2)}) async-start(), calls=%async_computation.3 | async-start | bytes 9437184 | tf_op jit(solution)/shard_map/reduce_scatter | solution.py:60
Sparse Core Ops, SparseCore 0:
  9.8 42.2 all-gather.9
  1025.2 213.5 reduce-scatter.4
  1241.4 57.4 reduce-scatter.2
